TPU v7x, 128 devices: a whole 4x4x4 slice. The times are simulated.
128 devices in a mesh: rows: 8 (over x, z_lo), cols: 16 (over z_hi, y, core).
Axes of the slice: x: 4, y: 4, z: 4 (z_hi: 2, z_lo: 2; z = z_hi * 2 + z_lo), core: 2. Of those that a mesh axis runs over, the one named last changes fastest.
Arguments:
- ancestor_inv: bfloat16 [16384, 16384], P('rows', 'cols'), may hold values from -0.0625 to 0.0625
- lfactor: bfloat16 [32, 256, 6, 256], P('cols'), may hold values from -0.8984375 to 0.8984375
- struct: int32 [6, 32], replicated, may hold values from 0 to 63, as said below
- validity: int32 [6, 32], replicated, may hold values from 0 to 1, as said below
- diag_inverse: float32 [6, 256, 256], replicated, may hold values from -6 to 6
Outputs:
- column_block: bfloat16 [16384, 1536], P(('rows', 'cols'))
- diagonal_block: float32 [6, 256, 256], replicated
Inputs may be any that keep to these rules, and one draw needn't show every extreme that they name: `struct`: within a supernode the 32 tile indices are distinct and increasing, and every list holds tiles 0 and 63. `validity`: every tile index of 0 to 63 is a valid entry of some supernode's list; some supernode has all 32 flags set.
All inputs are finite; a program needn't handle non-finite values.
Results may differ from a plain program's by a relative error of at most 0.001.
Values may be sent and summed in bfloat16 or wider, within the bound.
No kernel may reach another device: no remote copies, remote signals or barrier semaphores. Data moves between devices by JAX's collectives and lax.ppermute only.
A program may use at most 192 MiB of HBM per device.

v0:
```python
import jax
import jax.numpy as jnp
from jax import lax
from jax.sharding import PartitionSpec as P


def choose_tiles(tile_lists, flag_lists, first_tile, tile_count):
    wanted = first_tile + jnp.arange(tile_count, dtype=jnp.int32)
    hits = (tile_lists[:, :, None] == wanted[None, None, :]) & (flag_lists[:, :, None] > 0)
    return hits.astype(jnp.bfloat16)


def body(ancestor_inv, lfactor, struct, validity, diag_inverse):
    row_extent, col_extent = ancestor_inv.shape
    tile_size = lfactor.shape[1]
    super_count = lfactor.shape[2]
    row_tiles = row_extent // tile_size
    col_tiles = col_extent // tile_size
    slab_rows = row_extent // lax.axis_size("cols")
    row_index = lax.axis_index("rows")
    col_index = lax.axis_index("cols")
    col_first = col_index * col_tiles
    row_first = row_index * row_tiles
    global_start = row_index * row_extent + col_index * slab_rows
    own_tile = global_start // tile_size
    front_groups = (0, super_count)
    first_node, members = front_groups
    shard_piece = lax.all_gather(lfactor, "cols", axis=0, tiled=True)
    picker = choose_tiles(struct, validity, col_first, col_tiles)
    col_acc = jnp.einsum(
        "kpt,pakb->takb", picker, shard_piece, preferred_element_type=jnp.float32
    ).astype(jnp.bfloat16)
    row_picker = choose_tiles(struct, validity, row_first, row_tiles)
    row_acc = jnp.einsum(
        "kpt,pakb->takb", row_picker, shard_piece, preferred_element_type=jnp.float32
    )
    right_side = col_acc.reshape(col_extent, members * tile_size)
    products = -jnp.dot(ancestor_inv, right_side, preferred_element_type=jnp.float32)
    whole_rows = lax.psum(products, "cols")
    whole_updates = whole_rows.reshape(row_extent, members, tile_size)
    updates = lax.dynamic_slice_in_dim(whole_updates, col_index * slab_rows, slab_rows, 0)
    panel_slab = lax.dynamic_slice_in_dim(
        row_acc.reshape(row_extent, members, tile_size), col_index * slab_rows, slab_rows, 0
    )
    partial_value = jnp.einsum("akb,akc->kbc", panel_slab, updates, precision=lax.Precision.HIGHEST)
    diagonal_sum = lax.psum(partial_value, ("rows", "cols"))
    present = jnp.max(choose_tiles(struct, validity, own_tile, 1)[:, :, 0], axis=1).astype(
        jnp.float32
    )
    block_rows = (updates * present[None, :, None]).astype(jnp.bfloat16)
    diagonal = diag_inverse - diagonal_sum
    block_rows, diagonal = (block_rows, diagonal)
    column_block = block_rows.reshape(slab_rows, super_count * tile_size)
    return (column_block, diagonal)


def solution(mesh):
    return jax.shard_map(
        body,
        mesh=mesh,
        in_specs=(P("rows", "cols"), P("cols", None, None, None), P(), P(), P()),
        out_specs=(P(("rows", "cols"), None), P()),
        check_vma=False,
    )
```

profile of v0, /device:TPU:1, one launch (start us, length us, event | category | flops | bytes accessed | tf_op | source)
XLA Modules:
  0.0 557.4 jit_solution(9144877587433575651)
XLA Ops:
  7.2 0.0 all-gather.2.cloned.1.call-start
  7.2 0.7 all-gather.2.cloned.1.call-update
  7.9 0.0 all-reduce.3.cloned.1.call-start
  8.0 0.8 fusion.24
  8.8 153.8 %all-gather.2.cloned.1.call-done = bf16[32,256,6,256]{3,1,2,0:T(8,128)(2,1)} async-done(((bf16[2,256,6,256]{3,1,2,0:T(8,128)(2,1)}), bf16[32,256,6,256]{3,1,2,0:T(8,128)(2,1)}) %all-gather.2.cloned.1.call-update) | async-done | bytes 25165840 | tf_op jit(solution)/shard_map/all_gather | solution.py:28
  162.6 25.4 %convert_bitcast_fusion = bf16[4,256,6,256]{3,0,1,2:T(4,128)(2,1)} fusion(bf16[32,256,6,256]{3,1,2,0:T(8,128)(2,1)} %all-gather.2.cloned.1.call-done, s32[6,32]{1,0:T(8,128)} %param.7, s32[4]{0:T(128)S(1)} %iota_add_fusion.1, pred[6,32]{1,0:T(8,128)(4,1)S(1)} %get-tuple-element.7), kind=kOutput, calls=%fused_computation.6 | convolution fusion | flops 102237696 | bytes 28312528 | tf_op jit(solution)/shard_map/kpt,pakb->takb/dot_general | solution.py:30
  188.1 6.0 %copy.17 = bf16[4,256,6,256]{1,0,3,2:T(4,128)(2,1)S(1)} copy(bf16[4,256,6,256]{3,0,1,2:T(4,128)(2,1)} %convert_bitcast_fusion) | data formatting | bytes 6291456 | tf_op jit(solution)/shard_map/convert_element_type | solution.py:32
  194.1 0.8 copy.27
  194.8 11.6 %convolution_negate_fusion = f32[1536,2048]{1,0:T(8,128)} fusion(bf16[1024,1536]{0,1:T(8,128)(2,1)S(1)} %bitcast.29, bf16[2048,1024]{1,0:T(8,128)(2,1)} %param.5), kind=kOutput, calls=%fused_computation.4 | convolution fusion | flops 6445596672 | bytes 19922944 | tf_op jit(solution)/shard_map/dot_general | solution.py:38
  206.4 12.6 %copy.18 = f32[2048,6,256]{2,0,1:T(8,128)} copy(f32[2048,6,256]{0,2,1:T(8,128)} %bitcast.27) | data formatting | bytes 25165824 | tf_op jit(solution)/shard_map/reshape | solution.py:40
  219.0 0.0 copy-start.1
  219.0 0.0 all-reduce.3.cloned.1.call-update
  219.0 0.0 all-reduce.5.cloned.1.call-start
  219.1 0.6 copy-done.1
  219.7 26.8 %fusion.4 = f32[8,256,6,256]{3,0,1,2:T(8,128)} fusion(bf16[32,256,6,256]{3,1,2,0:T(8,128)(2,1)} %all-gather.2.cloned.1.call-done, s32[6,32]{1,0:T(8,128)S(1)} %copy-done.1, s32[8]{0:T(128)S(1)} %iota_add_fusion, pred[6,32]{1,0:T(8,128)(4,1)S(1)} %get-tuple-element.7), kind=kOutput, calls=%fused_computation.5 | convolution fusion | flops 201329664 | bytes 37749728 | tf_op jit(solution)/shard_map/kpt,pakb->takb/dot_general | solution.py:34
  246.5 0.0 copy-start
  246.5 13.4 %copy.21 = f32[8,256,6,256]{3,1,0,2:T(8,128)} copy(f32[8,256,6,256]{3,0,1,2:T(8,128)} %fusion.4) | data formatting | bytes 25165824 | tf_op jit(solution)/shard_map/kpt,pakb->takb/transpose | solution.py:34
  259.9 131.4 %all-reduce.3.cloned.1.call-done = f32[2048,6,256]{2,0,1:T(8,128)} async-done(((f32[2048,6,256]{2,0,1:T(8,128)}), f32[2048,6,256]{2,0,1:T(8,128)}) %all-reduce.3.cloned.1.call-update) | async-done | bytes 12582928 | tf_op jit(solution)/shard_map/psum | solution.py:39
  391.3 3.9 fusion.9
  395.3 0.0 all-reduce.5.cloned.1.call-update
  395.3 1.3 multiply_convert_fusion
  396.6 0.2 copy.19
  396.8 0.9 copy.23
  397.7 150.4 %all-reduce.5.cloned.1.call-done = f32[6,256,256]{2,1,0:T(8,128)} async-done(((f32[6,256,256]{2,1,0:T(8,128)}), f32[6,256,256]{2,1,0:T(8,128)}) %all-reduce.5.cloned.1.call-update) | async-done | bytes 1572880 | tf_op jit(solution)/shard_map/psum | solution.py:46
  548.1 0.0 copy-done
  548.1 2.8 sub.8
  (3 shorter events, 0.0 us)
Async XLA Ops:
  7.2 155.5 %all-gather.2.cloned.1.call-start = ((), (), s32[]{:S(2)}) async-start(), calls=%async_computation | async-start | bytes 26738688 | tf_op jit(solution)/shard_map/all_gather | solution.py:28
  7.9 383.4 %all-reduce.3.cloned.1.call-start = ((), (), s32[]{:S(2)}) async-start(), calls=%async_computation.1 | async-start | bytes 25165824 | tf_op jit(solution)/shard_map/psum | solution.py:39
  219.0 0.7 copy-start.1
  219.0 329.1 %all-reduce.5.cloned.1.call-start = ((), (), s32[]{:S(2)}) async-start(), calls=%async_computation.2 | async-start | bytes 3145728 | tf_op jit(solution)/shard_map/psum | solution.py:46
  246.5 301.6 %copy-start = (f32[6,256,256]{2,1,0:T(8,128)S(1)}, f32[6,256,256]{2,1,0:T(8,128)}, u32[]{:S(2)}) copy-start(f32[6,256,256]{2,1,0:T(8,128)} %param.9) | copy-start | bytes 4718596
Sparse Core Ops, SparseCore 0:
  10.4 152.1 all-gather.1
  219.1 172.1 all-reduce.2
  396.6 151.4 all-reduce.4
where the time goes:
time: 558 us; the launch traced here: 557 us
  waiting for transfers between devices  436 us (78%)
  matrix products  67.8 us (12%)
  local copies, waits for them, and re-layouts  34.5 us (6%)
  between operations  13.8 us (2%)
    all_gather x1, waiting for transfers between devices, body(): shard_piece = lax.all_gather(lfactor, 'cols', axis=0, tiled=True)  154 us
    psum x1, waiting for transfers between devices, body(): diagonal_sum = lax.psum(partial_value, ('rows', 'cols'))  150 us
    psum x1, waiting for transfers between devices, body(): whole_rows = lax.psum(products, 'cols')  131 us
    dot_general x1, matrix products, body(): jnp.einsum('kpt,pakb->takb', row_picker, shard_piece, preferred_element_t...  26.8 us
    dot_general x1, matrix products, body(): jnp.einsum('kpt,pakb->takb', picker, shard_piece, preferred_element_type=...  25.4 us
    transpose x1, local copies, waits for them, and re-layouts, body(): jnp.einsum('kpt,pakb->takb', row_picker, shard_piece, preferred_element_t...  13.4 us
    reshape x1, local copies, waits for them, and re-layouts, body(): whole_updates = whole_rows.reshape(row_extent, members, tile_size)  12.6 us
    dot_general x1, matrix products, body(): jnp.dot(ancestor_inv, right_side, preferred_element_type=jnp.float32)  11.6 us
  transfers between devices with their start and end apart: 3, of which 3 were waited for; matrix products, arithmetic and copies ran while one was open for 8% of the time, Pallas kernels for 0%

commit v1 on v0

v1 whole, which is shorter than its diff:
```python
import functools

import jax
import jax.numpy as jnp
from jax import lax
from jax.experimental import pallas as pl
from jax.experimental.pallas import tpu as pltpu
from jax.sharding import Mesh, PartitionSpec as P

BF16 = jnp.bfloat16
F32 = jnp.float32
NX, NL, NH, NY, NC = 4, 2, 2, 4, 2
XL = ("x", "l")
HY = ("h", "y")
CORE_SWAP = [(0, 1), (1, 0)]
LEVELS = 32000.0
LOWEST = -100.0


def pick_kernel(place, where, x_ref, o_ref):
    entries, _, width = x_ref.shape
    groups, slots = o_ref.shape[:2]
    window = slots - 1
    size = width // 3
    chip, core = where[0], where[1]
    for k in range(3):
        cols = slice(k * size, (k + 1) * size)

        def tile(t):
            p = place[core * 3 + k, t]
            block = x_ref[jnp.maximum(p, 0), :, cols]
            return jnp.where(p >= 0, block, jnp.zeros_like(block))

        for s in range(window):
            block = tile(chip * window + s)
            for g in range(groups):
                o_ref[g, s, :, cols] = block
        for g in range(groups):
            o_ref[g, window, :, cols] = tile(g * window + chip)


def product_kernel(where, own_ref, other_ref, l_ref, q_ref, panel):
    groups, slots, part, width = l_ref.shape
    window = slots - 1
    half = own_ref.shape[1]
    rows = own_ref.shape[0]

    @pl.when(pl.program_id(0) == 0)
    def _():
        for s in range(window):
            for g in range(groups):
                panel[pl.ds(s * groups * part + g * part, part), :] = l_ref[g, s]

    core = where[1]
    first = pl.multiple_of(core * half, half)
    second = pl.multiple_of((1 - core) * half, half)
    acc = jnp.dot(own_ref[...], panel[pl.ds(first, half), :], preferred_element_type=F32)
    acc += jnp.dot(other_ref[...], panel[pl.ds(second, half), :], preferred_element_type=F32)
    top = jnp.max(jnp.abs(acc), axis=0, keepdims=True)
    level = jnp.maximum(jnp.ceil(jnp.log2(jnp.maximum(top, 1e-37)) + 0.01), LOWEST)
    coded = jnp.round(acc * (jnp.exp2(-level) * LEVELS))
    q_ref[0, :rows, :] = coded.astype(jnp.int32).astype(jnp.int16)
    q_ref[0, rows:, :] = jnp.broadcast_to(level, (16, width)).astype(jnp.int32).astype(jnp.int16)


def finish_kernel(place, where, q_ref, l_ref, u_ref, d_ref):
    parts, _, width = q_ref.shape
    groups, slots, part, _ = l_ref.shape
    window = slots - 1
    rows = groups * part
    size = width // 3
    chip, core, group = where[0], where[1], where[2]
    mine = group * window + chip
    for k in range(3):
        cols = slice(k * size, (k + 1) * size)
        total = jnp.zeros((rows, size), F32)
        for j in range(parts):
            level = q_ref[j, rows : rows + 16, cols].astype(jnp.int32).astype(F32)[:1]
            total += q_ref[j, :rows, cols].astype(jnp.int32).astype(F32) * (
                jnp.exp2(level) * (1.0 / LEVELS)
            )
        update = -total
        keep = place[core * 3 + k, mine] >= 0
        u_ref[:, cols] = jnp.where(keep, update, jnp.zeros_like(update)).astype(BF16)
        own = jnp.concatenate([l_ref[g, slots - 1, :, cols] for g in range(groups)], axis=0)
        rest = update
        block = jnp.zeros((size, size), F32)
        for _ in range(3):
            high = rest.astype(BF16)
            rest = rest - high.astype(F32)
            block += lax.dot_general(
                own, high, (((0,), (0,)), ((), ())), preferred_element_type=F32
            )
        for i in range(2):
            d_ref[:, k * size + i * 128 : k * size + (i + 1) * 128] = block[:, i * 128 : (i + 1) * 128]


def body(ancestor_inv, lfactor, struct, validity, diag_inverse):
    rows, cols = ancestor_inv.shape
    entries, size, supers, _ = lfactor.shape
    groups = NX * NL
    chips = NH * NY
    part = size // groups
    width = supers // 2 * size
    group = lax.axis_index(XL)
    chip = lax.axis_index(HY)
    core = lax.axis_index("c")
    tiles = struct.shape[1] * 2
    window = tiles // chips
    smem = pl.BlockSpec(memory_space=pltpu.SMEM)
    vmem = pl.BlockSpec(memory_space=pltpu.VMEM)

    other = lax.ppermute(ancestor_inv, "c", CORE_SWAP)

    hits = (struct[:, :, None] == jnp.arange(tiles, dtype=jnp.int32)) & (validity[:, :, None] > 0)
    position = jnp.arange(struct.shape[1], dtype=jnp.int32)[None, :, None]
    place = jnp.max(jnp.where(hits, position, -1), axis=1)
    where = jnp.stack([chip, core, group]).astype(jnp.int32)

    share = lax.dynamic_slice_in_dim(lfactor, group * part, part, 1)
    share = share.reshape(entries, part, 2, width)
    share = jnp.transpose(share, (2, 0, 1, 3))
    share = jnp.broadcast_to(share[None], (chips, 2, entries, part, width))
    share = share.reshape(chips * 2, entries, part, width)
    share = lax.all_to_all(share, ("h", "y", "c"), split_axis=0, concat_axis=0, tiled=True)
    share = share.reshape(chips * 2 * entries, part, width)

    picked = pl.pallas_call(
        pick_kernel,
        out_shape=jax.ShapeDtypeStruct((groups, window + 1, part, width), BF16),
        in_specs=[smem, smem, vmem],
        out_specs=vmem,
        name="pick",
    )(place, where, share)
    picked = lax.all_to_all(picked, XL, split_axis=0, concat_axis=0, tiled=True)

    block = rows // chips
    coded = pl.pallas_call(
        product_kernel,
        grid=(chips,),
        out_shape=jax.ShapeDtypeStruct((chips, block + 16, width), jnp.int16),
        in_specs=[
            smem,
            pl.BlockSpec((block, cols), lambda i: (i, 0)),
            pl.BlockSpec((block, cols), lambda i: (i, 0)),
            vmem,
        ],
        out_specs=pl.BlockSpec((1, block + 16, width), lambda i: (i, 0, 0)),
        scratch_shapes=[pltpu.VMEM((2 * cols, width), BF16)],
        name="product",
    )(where, ancestor_inv, other, picked)
    coded = lax.all_to_all(coded, HY, split_axis=0, concat_axis=0, tiled=True)

    updates, diag = pl.pallas_call(
        finish_kernel,
        out_shape=[
            jax.ShapeDtypeStruct((block, width), BF16),
            jax.ShapeDtypeStruct((size, width), F32),
        ],
        in_specs=[smem, smem, vmem, vmem],
        out_specs=[vmem, vmem],
        name="finish",
    )(place, where, coded, picked)

    slab = block // 2
    mine = lax.dynamic_slice_in_dim(updates, core * slab, slab, 0)
    theirs = lax.dynamic_slice_in_dim(updates, (1 - core) * slab, slab, 0)
    theirs = lax.ppermute(theirs, "c", CORE_SWAP)
    column_block = jnp.where(
        core == 0,
        jnp.concatenate([mine, theirs], axis=1),
        jnp.concatenate([theirs, mine], axis=1),
    )

    pieces = groups * chips
    diag = diag.reshape(pieces, size // pieces, width)
    diag = lax.all_to_all(diag, ("x", "l", "h", "y"), split_axis=0, concat_axis=0, tiled=True)
    piece = jnp.sum(diag, axis=0)
    piece = jnp.broadcast_to(piece[None], (pieces * 2,) + piece.shape)
    whole = lax.all_to_all(piece, ("x", "l", "h", "y", "c"), split_axis=0, concat_axis=0, tiled=True)
    whole = whole.reshape(pieces, 2, size // pieces, supers // 2, size)
    whole = jnp.transpose(whole, (1, 3, 0, 2, 4)).reshape(supers, size, size)
    return column_block, diag_inverse - whole


def solution(mesh):
    fine = Mesh(mesh.devices.reshape(NX, NL, NH, NY, NC), ("x", "l", "h", "y", "c"))
    return jax.shard_map(
        body,
        mesh=fine,
        in_specs=(P(XL, ("h", "y", "c")), P(("h", "y", "c")), P(), P(), P()),
        out_specs=(P(("x", "l", "h", "y", "c")), P()),
        check_vma=False,
    )
```

time: 558 us -> 223 us (0.40)
  waiting for transfers between devices: 436 us -> 91.5 us
  matrix products: 67.8 us -> 0 us
  blocking collectives: 0 us -> 61.5 us
  starting transfers between devices: 0.12 us -> 22.9 us
  Pallas kernels: 0 us -> 21.8 us
  local copies, waits for them, and re-layouts: 34.5 us -> 17.3 us
  between operations: 13.8 us -> 0.72 us
    psum x2 -> x0, waiting for transfers between devices: 282 us -> none  [the longest x1 150 us: body(): diagonal_sum = lax.psum(partial_value, ('rows', 'cols'))]
    all_gather x1 -> x0, waiting for transfers between devices: 154 us -> none  [body(): shard_piece = lax.all_gather(lfactor, 'cols', axis=0, tiled=True)]
    all_to_all x0 -> x3, waiting for transfers between devices: none -> 90.3 us  [the longest x1 50.1 us: body(): picked = lax.all_to_all(picked, XL, split_axis=0, concat_axis=0, tiled=True)]
    dot_general x4 -> x0, matrix products: 67.8 us -> none  [the longest x1 26.8 us: body(): jnp.einsum('kpt,pakb->takb', row_picker, shard_piece, preferred_element_t...]
    all_to_all x0 -> x2, blocking collectives: none -> 61.5 us  [the longest x1 44.9 us: body(): coded = lax.all_to_all(coded, HY, split_axis=0, concat_axis=0, tiled=True)]
    pallas_call x0 -> x3, Pallas kernels: none -> 21.8 us  [the longest x1 13 us: body(): pl.pallas_call(product_kernel, grid=(chips,), out_shape=jax.ShapeDtypeStr...]
    all_to_all x0 -> x3, starting transfers between devices: none -> 21.5 us  [the longest x1 9.42 us: body(): lax.all_to_all(share, ('h', 'y', 'c'), split_axis=0, concat_axis=0, tiled...]
    transpose x1 -> x2, local copies, waits for them, and re-layouts: 13.4 us -> 2.63 us  [the longest x1 2.6 us: body(): whole = jnp.transpose(whole, (1, 3, 0, 2, 4)).reshape(supers, size, size)]
  transfers between devices with their start and end apart: 3 -> 5, of which waited for: 3 -> 4; matrix products, arithmetic and copies ran while one was open for 8% -> 2% of each run, Pallas kernels for 0% -> 2%
where the time goes in v1:
time: 223 us; the launch traced here: 222 us
  waiting for transfers between devices  91.5 us (41%)
  blocking collectives  61.5 us (28%)
  starting transfers between devices  22.9 us (10%)
  Pallas kernels  21.8 us (10%)
  local copies, waits for them, and re-layouts  17.3 us (8%)
  other arithmetic  6.58 us (3%)
    all_to_all x1, waiting for transfers between devices, body(): picked = lax.all_to_all(picked, XL, split_axis=0, concat_axis=0, tiled=True)  50.1 us
    all_to_all x1, blocking collectives, body(): coded = lax.all_to_all(coded, HY, split_axis=0, concat_axis=0, tiled=True)  44.9 us
    all_to_all x1, waiting for transfers between devices, body(): lax.all_to_all(share, ('h', 'y', 'c'), split_axis=0, concat_axis=0, tiled...  21.3 us
    all_to_all x1, waiting for transfers between devices, body(): lax.all_to_all(piece, ('x', 'l', 'h', 'y', 'c'), split_axis=0, concat_axi...  18.8 us
    all_to_all x1, blocking collectives, body(): lax.all_to_all(diag, ('x', 'l', 'h', 'y'), split_axis=0, concat_axis=0, t...  16.7 us
    pallas_call x1, Pallas kernels, body(): pl.pallas_call(product_kernel, grid=(chips,), out_shape=jax.ShapeDtypeStr...  13 us
    all_to_all x1, starting transfers between devices, body(): lax.all_to_all(share, ('h', 'y', 'c'), split_axis=0, concat_axis=0, tiled...  9.42 us
    all_to_all x1, starting transfers between devices, body(): lax.all_to_all(piece, ('x', 'l', 'h', 'y', 'c'), split_axis=0, concat_axi...  7.56 us
  transfers between devices with their start and end apart: 5, of which 4 were waited for; matrix products, arithmetic and copies ran while one was open for 2% of the time, Pallas kernels for 2%

profile of v1, /device:TPU:1, one launch (start us, length us, event | category | flops | bytes accessed | tf_op | source)
XLA Modules:
  0.0 222.3 jit_solution(10809571243673331590)
XLA Ops:
  0.6 0.0 copy-start
  0.7 1.4 copy-done
  2.1 0.1 copy.16
  2.2 0.1 reshape.27
  2.4 1.3 broadcast_in_dim.18
  3.7 0.0 copy-start.2
  3.7 0.0 copy-start.3
  3.7 9.4 %all-to-all-start = ((bf16[16,2,32,768]{3,2,1,0:T(8,128)(2,1)}), bf16[16,2,32,768]{3,2,1,0:T(8,128)(2,1)S(1)}, u32[]{:S(2)}, u32[]{:S(2)}) async-start(bf16[16,2,32,768]{3,2,1,0:T(8,128)(2,1)} %bitcast.4), calls=%async_computation | async-start | bytes 3145728 | tf_op jit(solution)/shard_map/all_to_all | solution.py:125
  13.1 0.2 collective-permute-start
  13.3 0.6 pad_add_fusion.where
  13.9 0.0 copy-done.2
  13.9 0.0 copy-done.3
  13.9 0.7 select_reduce_fusion.place
  14.6 21.3 %all-to-all-done = bf16[16,2,32,768]{3,2,1,0:T(8,128)(2,1)S(1)} async-done(((bf16[16,2,32,768]{3,2,1,0:T(8,128)(2,1)}), bf16[16,2,32,768]{3,2,1,0:T(8,128)(2,1)S(1)}, u32[]{:S(2)}, u32[]{:S(2)}) %all-to-all-start) | async-done | bytes 1572896 | tf_op jit(solution)/shard_map/all_to_all | solution.py:125
  36.0 0.0 copy-start.1
  36.0 1.1 copy-done.1
  37.1 3.5 %pick.1 = bf16[8,9,32,768]{3,2,1,0:T(8,128)(2,1)} custom-call(s32[6,64]{1,0:T(8,128)} %select_reduce_fusion.place, s32[3]{0:T(128)} %pad_add_fusion.where, bf16[32,32,768]{2,1,0:T(8,128)(2,1)} %bitcast.10), custom_call_target="tpu_custom_call" | custom-call | tf_op jit(solution)/shard_map/pick/pallas_call | solution.py:128
  40.7 4.5 %all-to-all-start.1 = ((bf16[8,9,32,768]{3,2,1,0:T(8,128)(2,1)}), bf16[8,9,32,768]{3,2,1,0:T(8,128)(2,1)}, u32[]{:S(2)}, u32[]{:S(2)}) async-start(bf16[8,9,32,768]{3,2,1,0:T(8,128)(2,1)} %pick.1), calls=%async_computation.1 | async-start | bytes 7077888 | tf_op jit(solution)/shard_map/all_to_all | solution.py:135
  45.2 0.0 collective-permute-done.other_ref
  45.2 50.1 %all-to-all-done.1.l_ref = bf16[8,9,32,768]{3,2,1,0:T(8,128)(2,1)} async-done(((bf16[8,9,32,768]{3,2,1,0:T(8,128)(2,1)}), bf16[8,9,32,768]{3,2,1,0:T(8,128)(2,1)}, u32[]{:S(2)}, u32[]{:S(2)}) %all-to-all-start.1) | async-done | bytes 3538976 | tf_op jit(solution)/shard_map/all_to_all | solution.py:135
  95.3 13.0 %product.1 = s16[8,272,768]{2,1,0:T(8,128)(2,1)} custom-call(s32[3]{0:T(128)} %pad_add_fusion.where, bf16[2048,1024]{1,0:T(8,128)(2,1)} %own_ref.1, bf16[2048,1024]{1,0:T(8,128)(2,1)} %collective-permute-done.other_ref, bf16[8,9,32,768]{3,2,1,0:T(8,128)(2,1)} %all-to-all-done.1.l_ref), custom_call_target="tpu_custom_call" | custom-call | tf_op jit(solution)/shard_map/product/pallas_call | solution.py:138
  108.3 44.9 %all_to_all.25.q_ref = s16[8,272,768]{2,1,0:T(8,128)(2,1)} all-to-all(s16[8,272,768]{2,1,0:T(8,128)(2,1)} %product.1), channel_id=1, replica_groups=mesh['x'=4,'l'=2,'h'=2,'y'=4,'c'=2] {'h','y'}, dimensions={0} | all-to-all | bytes 6684672 | tf_op jit(solution)/shard_map/all_to_all | solution.py:152
  153.2 5.3 %finish.1 = (bf16[256,768]{1,0:T(8,128)(2,1)}, f32[256,768]{1,0:T(8,128)}) custom-call(s32[6,64]{1,0:T(8,128)} %select_reduce_fusion.place, s32[3]{0:T(128)} %pad_add_fusion.where, s16[8,272,768]{2,1,0:T(8,128)(2,1)} %all_to_all.25.q_ref, bf16[8,9,32,768]{3,2,1,0:T(8,128)(2,1)} %all-to-all-done.1.l_ref), custom_call_target="tpu_custom_call" | custom-call | tf_op jit(solution)/shard_map/finish/pallas_call | solution.py:154
  158.4 1.4 reshape.30
  159.8 16.7 %all_to_all.26 = f32[64,4,768]{2,1,0:T(4,128)S(1)} all-to-all(f32[64,4,768]{2,1,0:T(4,128)S(1)} %reshape.30), channel_id=1, replica_groups=mesh['x'=4,'l'=2,'h'=2,'y'=4,'c'=2] {'x','l','h','y'}, dimensions={0} | all-to-all | bytes 1572864 | tf_op jit(solution)/shard_map/all_to_all | solution.py:177
  176.4 0.2 reduce_sum.9
  176.6 1.3 broadcast_in_dim.19
  177.9 7.6 %all-to-all-start.4 = ((f32[128,4,768]{2,1,0:T(4,128)}), f32[128,4,768]{2,1,0:T(4,128)S(1)}, u32[]{:S(2)}, u32[]{:S(2)}) async-start(f32[128,4,768]{2,1,0:T(4,128)} %broadcast_in_dim.19), calls=%async_computation.4 | async-start | bytes 3145728 | tf_op jit(solution)/shard_map/all_to_all | solution.py:180
  185.5 1.1 constant_dynamic-slice_fusion.1
  186.6 1.3 collective-permute-start.1
  187.8 1.2 collective-permute-done.1
  189.0 1.9 maximum_select_fusion
  190.9 18.8 %all-to-all-done.4 = f32[128,4,768]{2,1,0:T(4,128)S(1)} async-done(((f32[128,4,768]{2,1,0:T(4,128)}), f32[128,4,768]{2,1,0:T(4,128)S(1)}, u32[]{:S(2)}, u32[]{:S(2)}) %all-to-all-start.4) | async-done | bytes 1572896 | tf_op jit(solution)/shard_map/all_to_all | solution.py:180
  209.7 1.4 copy.18
  211.1 3.7 %reshape.31 = f32[64,2,4,3,256]{4,3,1,0,2:T(4,128)} reshape(f32[128,4,768]{2,0,1:T(8,128)} %copy.18) | data formatting | bytes 3145728 | tf_op jit(solution)/shard_map/reshape | solution.py:181
  214.8 2.6 %copy.19 = f32[2,3,64,4,256]{4,3,2,1,0:T(4,128)S(1)} copy(f32[2,3,64,4,256]{4,1,0,2,3:T(4,128)} %bitcast.9) | data formatting | bytes 3145728 | tf_op jit(solution)/shard_map/transpose | solution.py:182
  217.4 1.7 reshape.32
  219.1 3.2 %sub.7 = f32[6,256,256]{2,1,0:T(8,128)} subtract(f32[6,256,256]{2,1,0:T(8,128)} %param.9, f32[6,256,256]{2,1,0:T(8,128)} %reshape.32) | non-fusion elementwise | flops 393216 | bytes 4718592 | tf_op jit(solution)/shard_map/sub | solution.py:183
  (3 shorter events, 0.0 us)
Async XLA Ops:
  0.6 1.4 copy-start
  3.7 10.2 %copy-start.2 = (s32[6,32]{1,0:T(8,128)S(1)}, s32[6,32]{1,0:T(8,128)}, u32[]{:S(2)}) copy-start(s32[6,32]{1,0:T(8,128)} %param.8) | copy-start | bytes 2308
  3.7 10.2 %copy-start.3 = (s32[6,32]{1,0:T(8,128)S(1)}, s32[6,32]{1,0:T(8,128)}, u32[]{:S(2)}) copy-start(s32[6,32]{1,0:T(8,128)} %param.7) | copy-start | bytes 2308
  3.7 32.3 %all-to-all-start = ((bf16[16,2,32,768]{3,2,1,0:T(8,128)(2,1)}), bf16[16,2,32,768]{3,2,1,0:T(8,128)(2,1)S(1)}, u32[]{:S(2)}, u32[]{:S(2)}) async-start(bf16[16,2,32,768]{3,2,1,0:T(8,128)(2,1)} %bitcast.4), calls=%async_computation | async-start | bytes 3145728 | tf_op jit(solution)/shard_map/all_to_all | solution.py:125
  13.1 32.1 %collective-permute-start = (bf16[2048,1024]{1,0:T(8,128)(2,1)}, bf16[2048,1024]{1,0:T(8,128)(2,1)}, u32[]{:S(2)}, u32[]{:S(2)}) collective-permute-start(bf16[2048,1024]{1,0:T(8,128)(2,1)} %own_ref.1), channel_id=1, source_target_pairs={{0,1},{1,0},{2,3},{3,2},{4,5},{5,4},{6,7},{7,6},{8,9},{9,8},{10,11... | collective-permute-start | bytes 12582920 | tf_op jit(solution)/shard_map/ppermute | solution.py:113
  36.0 1.1 copy-start.1
  40.7 54.6 %all-to-all-start.1 = ((bf16[8,9,32,768]{3,2,1,0:T(8,128)(2,1)}), bf16[8,9,32,768]{3,2,1,0:T(8,128)(2,1)}, u32[]{:S(2)}, u32[]{:S(2)}) async-start(bf16[8,9,32,768]{3,2,1,0:T(8,128)(2,1)} %pick.1), calls=%async_computation.1 | async-start | bytes 7077888 | tf_op jit(solution)/shard_map/all_to_all | solution.py:135
  177.9 31.8 %all-to-all-start.4 = ((f32[128,4,768]{2,1,0:T(4,128)}), f32[128,4,768]{2,1,0:T(4,128)S(1)}, u32[]{:S(2)}, u32[]{:S(2)}) async-start(f32[128,4,768]{2,1,0:T(4,128)} %broadcast_in_dim.19), calls=%async_computation.4 | async-start | bytes 3145728 | tf_op jit(solution)/shard_map/all_to_all | solution.py:180
  186.6 2.5 %collective-permute-start.1 = (bf16[128,768]{1,0:T(8,128)(2,1)S(1)}, bf16[128,768]{1,0:T(8,128)(2,1)}, u32[]{:S(2)}, u32[]{:S(2)}) collective-permute-start(bf16[128,768]{1,0:T(8,128)(2,1)S(1)} %get-tuple-element.7), channel_id=1, source_target_pairs={{0,1},{1,0},{2,3},{3,2},{4,5},{5,4},{6,7},{7,6},{8,9},{9,8},{10,11... | collective-permute-start | bytes 589832 | tf_op jit(solution)/shard_map/ppermute | solution.py:168
